TPU v7x, 32 devices: a whole 2x2x4 slice. The times are simulated.
32 devices in a mesh: pole: 2 (over x), row: 8 (over z, y), col: 2 (over core).
Axes of the slice: x: 2, y: 2, z: 4, core: 2. Of those that a mesh axis runs over, the one named last changes fastest.
Arguments:
- inverse_pairs: bfloat16 [4, 12288, 12288], P('pole', 'row', 'col'), parts along dimension 0, may hold values from -0.09375 to 0.09375
- factor_rows: bfloat16 [4, 2, 2048, 256], P('pole', None, 'row', 'col'), parts along dimension 0, may hold values from -1.1953125 to 1.1953125
- diag_blocks: bfloat16 [4, 2, 256, 256], P('pole', None, None, 'col'), parts along dimension 0, may hold values from -6 to 6
- row_lists: int32 [2, 16], replicated, may hold values from 0 to 95, as said below
- block_order: int32 [96], replicated, may hold values from 0 to 95, each once
Outputs:
- inv_cols: float32 [4, 2, 12288, 256], P('pole', None, 'row', 'col'), parts along dimension 0
- schur_blocks: float32 [4, 2, 256, 256], P('pole', None, None, 'col'), parts along dimension 0
There are 2 independent parts, one for each index of `pole`. A program takes and returns all parts, laid end to end along the dimension named above; an argument that names none is the same for every part. Nothing has to cross between parts.
Inputs may be any that keep to these rules, and one draw needn't show every extreme that they name: `row_lists`: each of the 2 rows holds 16 different block numbers in increasing order, always including 0 and 95.
All inputs are finite; a program needn't handle non-finite values.
Results may differ from a plain program's by a relative error of at most 0.0003.
Values may be sent and summed in bfloat16 or wider, within the bound.
A program may use at most 128 MiB of HBM per device.

v0:
```python
import functools

import jax
import jax.numpy as jnp
from jax import lax
from jax.experimental import pallas as pl
from jax.experimental.pallas import tpu as pltpu
from jax.sharding import PartitionSpec as P

NSN = 2
BLK = 128
MESH = pl.DeviceIdType.MESH
ANY = pl.BlockSpec(memory_space=pl.ANY)
VMEM = pl.BlockSpec(memory_space=pltpu.VMEM)
SMEM = pl.BlockSpec(memory_space=pltpu.SMEM)


def aligned(start, size):
    return pl.ds(pl.multiple_of(start, size), size)


def kernel(n, ny, pick, keep, local_pick, local_keep, x_ref, a_ref, out_ref, sum_ref,
           a_buf, g_ref, own, oth, recv, bbuf, mine, parts,
           a_sem, loc_sem, z_send, z_recv, y_send, y_recv, s_send, s_recv,
           v_send, v_recv, o_sem, r_send, r_recv, b_send, b_recv):
    nz = n // ny
    span = g_ref.shape[3] * BLK // n
    rows = a_ref.shape[1]
    blocks_col = a_ref.shape[2] // BLK
    blocks_row = rows // BLK
    tile = 512 if rows % 512 == 0 else 384 if rows % 384 == 0 else BLK
    per = max(1, span // BLK)
    unit = min(span, BLK)
    row = lax.axis_index("row")
    col = lax.axis_index("col")
    z = row // ny
    y = row % ny
    oy = ny - 1 - y
    sibling = {"col": 1 - col}
    up = {"row": row + ny}
    down = {"row": row - ny}
    across = {"row": z * ny + oy}

    def stream(b):
        return pltpu.make_async_copy(a_ref.at[:, :, aligned(b * BLK, BLK)], a_buf.at[b], a_sem.at[b])

    def start_stream(b, carry):
        stream(b).start()
        return carry

    def wait_stream(b, carry):
        stream(b).wait()
        return carry

    def slot(c, r):
        if span >= BLK:
            return g_ref.at[c, :, :, pl.ds(r * per, per)]
        return g_ref.at[c, :, :, r * span // BLK, aligned(r * span % BLK, span)]

    local = pltpu.make_async_copy(x_ref, slot(col, row), loc_sem)
    local.start()

    barrier = pltpu.get_barrier_semaphore()
    pl.semaphore_signal(barrier, inc=1, device_id=sibling, device_id_type=MESH)
    for d in range(1, n):
        pl.semaphore_signal(barrier, inc=1, device_id={"row": (row + d) % n}, device_id_type=MESH)
    pl.semaphore_wait(barrier, n)

    def copy(src, c, r, send, got, target):
        return pltpu.make_async_remote_copy(
            src_ref=src, dst_ref=slot(c, r), send_sem=send, recv_sem=got,
            device_id=target, device_id_type=MESH)

    def line(src, zz, target):
        return copy(src, col, zz * ny + y, z_send.at[zz], z_recv.at[zz], target)

    def side(src, zz, yy):
        return copy(src, col, zz * ny + yy, y_send.at[zz], y_recv.at[zz], across)

    def sib(src, c, r):
        return copy(src, c, r, s_send.at[r], s_recv.at[r], sibling)

    def here(zz, yy):
        return slot(col, zz * ny + yy)

    first_up = copy(x_ref, col, row, z_send.at[nz], z_recv.at[z], up)
    first_down = copy(x_ref, col, row, z_send.at[nz + 1], z_recv.at[z], down)
    pl.when(z < nz - 1)(lambda: first_up.start())
    pl.when(z > 0)(lambda: first_down.start())
    side(x_ref, z, y).start()
    sib(x_ref, col, row).start()
    lax.fori_loop(0, blocks_col, start_stream, 0)
    own[...] = jnp.zeros_like(own)
    oth[...] = jnp.zeros_like(oth)
    mine[...] = jnp.zeros_like(mine)
    local.wait()

    def from_line(zz, forward, target):
        line(here(zz, y), zz, target).wait_recv()

        @pl.when(forward)
        def _():
            line(here(zz, y), zz, target).start()

        side(here(zz, y), zz, y).start()
        sib(here(zz, y), col, zz * ny + y).start()

    def from_side(zz):
        side(here(zz, oy), zz, oy).wait_recv()
        sib(here(zz, oy), col, zz * ny + oy).start()

    outs = (own, oth)

    def multiply(r):
        sib(slot(1 - col, r), 1 - col, r).wait_recv()

        def supernode(k, carry):
            if unit < BLK:
                bbuf[...] = jnp.zeros_like(bbuf)
            for e in range(per):
                start = r * span + e * BLK
                scale = keep[k, start // BLK]
                base = e * 2 * BLK
                if unit < BLK:
                    shift = start % BLK
                    top = aligned(base + shift, unit)
                    low = aligned(base + BLK + shift, unit)
                else:
                    top = pl.ds(base, unit)
                    low = pl.ds(base + BLK, unit)
                for rel in range(2):
                    c = col if rel == 0 else 1 - col
                    at = pl.ds(0, unit) if unit == BLK else aligned(start % BLK, unit)
                    real = (g_ref[c, k, 0, start // BLK, at, :].astype(jnp.float32) * scale).astype(jnp.bfloat16)
                    imag = (g_ref[c, k, 1, start // BLK, at, :].astype(jnp.float32) * scale).astype(jnp.bfloat16)
                    left = rel * 2 * BLK
                    bbuf[top, left:left + BLK] = -real
                    bbuf[top, left + BLK:left + 2 * BLK] = -imag
                    bbuf[low, left:left + BLK] = imag
                    bbuf[low, left + BLK:left + 2 * BLK] = -real

            def by_tile(t, inner):
                at = aligned(t * tile, tile)
                pieces = []
                for e in range(per):
                    block = pick[k, (r * span + e * BLK) // BLK]
                    pieces += [a_buf[block, 0, at, :], a_buf[block, 1, at, :]]
                left = jnp.concatenate(pieces, axis=1)
                for rel in range(2):
                    found = jnp.dot(left, bbuf[:, rel * 2 * BLK:(rel + 1) * 2 * BLK],
                                    preferred_element_type=jnp.float32)
                    outs[rel][k, 0, at, :] += found[:, :BLK]
                    outs[rel][k, 1, at, :] += found[:, BLK:]
                return inner

            lax.fori_loop(0, rows // tile, by_tile, 0)
            return carry

        lax.fori_loop(0, NSN, supernode, 0)

    def one_round(d, carry):
        pl.when(z - d >= 0)(lambda: from_line(z - d, z < nz - 1, up))
        pl.when(z + d < nz)(lambda: from_line(z + d, z > 0, down))
        pl.when(z - d + 1 >= 0)(lambda: from_side(z - d + 1))
        pl.when((d > 1) & (z + d - 1 < nz))(lambda: from_side(z + d - 1))

        @pl.when(d == 2)
        def _():
            lax.fori_loop(0, blocks_col, wait_stream, 0)


        def late(q, inner):
            away = d - 2 - q // 2
            zz = z + jnp.where(q % 2 == 0, -away, away)
            yy = jnp.where(q // 2 == 0, y, oy)
            valid = (away >= 0) & (zz >= 0) & (zz < nz) & ((away > 0) | (q % 2 == 0))
            pl.when(valid)(lambda: multiply(zz * ny + yy))
            return inner

        lax.fori_loop(0, 4, late, 0)
        return carry

    lax.fori_loop(1, nz + 3, one_round, 0)

    def swap(k):
        return pltpu.make_async_remote_copy(
            src_ref=oth.at[k], dst_ref=recv.at[k], send_sem=v_send.at[k], recv_sem=v_recv.at[k],
            device_id=sibling, device_id_type=MESH)

    for k in range(NSN):
        swap(k).start()
    for r in range(n):
        sib(slot(col, r), col, r).wait_send()
    for zz in range(nz):
        side(here(zz, y), zz, y).wait_send()
        pl.when(((zz < z) & (z < nz - 1)) | ((zz > z) & (z > 0)))(
            lambda: line(here(zz, y), zz, up).wait_send())
    pl.when(z < nz - 1)(lambda: first_up.wait_send())
    pl.when(z > 0)(lambda: first_down.wait_send())

    size = sum_ref.shape[0] // (NSN * n)

    def place(k, r):
        return aligned(k * n * size + r * size, size)

    def scatter(k, d):
        to = (row + d) % n
        return pltpu.make_async_remote_copy(
            src_ref=mine.at[place(k, to)], dst_ref=parts.at[k, d],
            send_sem=r_send.at[k, d], recv_sem=r_recv.at[k, d],
            device_id={"row": to}, device_id_type=MESH)

    def spread(k, d):
        return pltpu.make_async_remote_copy(
            src_ref=parts.at[k, 0], dst_ref=sum_ref.at[place(k, row)],
            send_sem=b_send.at[k, d], recv_sem=b_recv.at[k, d],
            device_id={"row": (row + d) % n}, device_id_type=MESH)

    group = 3 if blocks_row % 3 == 0 else 1
    width = 2 * BLK
    for k in range(NSN):
        swap(k).wait_recv()
        own[k] += recv[k]
        pltpu.make_async_copy(own.at[k], out_ref.at[k], o_sem.at[k]).start()

        def correct(s, carry, k=k):
            left, right = [], []
            for u in range(group):
                t = s * group + u
                j = local_pick[k, t]
                scale = local_keep[k, t]
                for p in range(2):
                    left.append(jnp.concatenate([g_ref[0, k, p, j], g_ref[1, k, p, j]], axis=1))
                real = own[k, 0, aligned(t * BLK, BLK), :] * scale
                imag = own[k, 1, aligned(t * BLK, BLK), :] * scale
                right.append(jnp.concatenate([real, imag], axis=1))
                right.append(jnp.concatenate([-imag, real], axis=1))
            factor = jnp.concatenate(left, axis=0)
            wide = jnp.concatenate(right, axis=0)
            total = None
            for _ in range(2):
                piece = wide.astype(jnp.bfloat16)
                wide = wide - piece.astype(jnp.float32)
                term = lax.dot_general(factor, piece, (((0,), (0,)), ((), ())),
                                       preferred_element_type=jnp.float32)
                total = term if total is None else total + term
            mine[2 * k * width:(2 * k + 1) * width, :] += total[:, :BLK]
            mine[(2 * k + 1) * width:(2 * k + 2) * width, :] += total[:, BLK:]
            return carry

        lax.fori_loop(0, blocks_row // group, correct, 0)
        for d in range(1, n):
            scatter(k, d).start()


    for k in range(NSN):
        total = mine[place(k, row), :]
        for d in range(1, n):
            scatter(k, d).wait_recv()
            total = total + parts[k, d]
        parts[k, 0] = total
        sum_ref[place(k, row), :] = total
        for d in range(1, n):
            spread(k, d).start()
    for k in range(NSN):
        swap(k).wait_send()
        pltpu.make_async_copy(own.at[k], out_ref.at[k], o_sem.at[k]).wait()
        for d in range(1, n):
            scatter(k, d).wait_send()
            spread(k, d).wait()


def local(n, inverse_pairs, factor_rows, diag_blocks, row_lists, block_order):
    rows, cols = inverse_pairs.shape[1:]
    blocks_row, blocks_col = rows // BLK, cols // BLK
    listed = row_lists.shape[1]
    hits = row_lists[:, :, None] == block_order[None, None, :]
    storage = jnp.arange(block_order.shape[0], dtype=jnp.int32)
    position = jnp.sum(jnp.where(hits, storage, 0), axis=2).astype(jnp.int32)
    pick = position - lax.axis_index("col") * blocks_col
    keep = ((pick >= 0) & (pick < blocks_col)).astype(jnp.float32)
    pick = jnp.clip(pick, 0, blocks_col - 1)
    place = lax.axis_index("row") * blocks_row + jnp.arange(blocks_row, dtype=jnp.int32)
    found = position[:, None, :] == place[None, :, None]
    local_pick = jnp.sum(jnp.where(found, jnp.arange(listed, dtype=jnp.int32), 0), axis=2).astype(jnp.int32)
    local_keep = jnp.sum(found.astype(jnp.float32), axis=2)

    ny = 2 if n % 2 == 0 else 1
    nz = n // ny
    span, half = factor_rows.shape[2:]
    size = NSN * 2 * 2 * half
    per = max(1, span // BLK)
    shards = factor_rows.reshape(NSN, 2, per, BLK, half) if span >= BLK else factor_rows
    dma = pltpu.SemaphoreType.DMA
    side = (NSN, 2, rows, half)
    values, correction = pl.pallas_call(
        functools.partial(kernel, n, ny),
        out_shape=(jax.ShapeDtypeStruct(side, jnp.float32), jax.ShapeDtypeStruct((size, half), jnp.float32)),
        in_specs=[SMEM, SMEM, SMEM, SMEM, ANY, ANY],
        out_specs=(ANY, VMEM),
        scratch_shapes=[
            pltpu.VMEM((blocks_col, 2, rows, BLK), jnp.bfloat16),
            pltpu.VMEM((2, NSN, 2, listed, BLK, half), jnp.bfloat16),
            pltpu.VMEM(side, jnp.float32),
            pltpu.VMEM(side, jnp.float32),
            pltpu.VMEM(side, jnp.float32),
            pltpu.VMEM((per * 2 * BLK, 4 * BLK), jnp.bfloat16),
            pltpu.VMEM((size, half), jnp.float32),
            pltpu.VMEM((NSN, n, size // (NSN * n), half), jnp.float32),
            dma((blocks_col,)), dma, dma((nz + 2,)), dma((nz,)), dma((nz,)), dma((nz,)), dma((n,)), dma((n,)),
            dma((NSN,)), dma((NSN,)), dma((NSN,)), dma((NSN, n)), dma((NSN, n)), dma((NSN, n)), dma((NSN, n)),
        ],
        compiler_params=pltpu.CompilerParams(
            collective_id=0, has_side_effects=True, vmem_limit_bytes=66000000),
        name="inversion_step",
    )(pick, keep, local_pick, local_keep, shards, inverse_pairs)
    schur = diag_blocks.astype(jnp.float32) - correction.reshape(diag_blocks.shape)
    return (values, schur)


def solution(mesh):
    in_specs = (
        P("pole", "row", "col"),
        P("pole", None, "row", "col"),
        P("pole", None, None, "col"),
        P(),
        P(),
    )
    out_specs = (P("pole", None, "row", "col"), P("pole", None, None, "col"))
    return jax.shard_map(functools.partial(local, mesh.shape["row"]), mesh=mesh, in_specs=in_specs,
                         out_specs=out_specs, check_vma=False)
```

profile of v0, /device:TPU:0, one launch (start us, length us, event | category | flops | bytes accessed | tf_op | source)
XLA Modules:
  0.0 85.5 jit_solution(8461332454575901663)
XLA Ops:
  0.6 0.9 %select_reduce_fusion = s32[2,16]{1,0:T(2,128)S(1)} fusion(s32[96]{0:T(128)} %param.9, s32[2,16]{1,0:T(2,128)} %param.8), kind=kLoop, calls=%fused_computation.3 | loop fusion | flops 9184 | bytes 640 | tf_op jit(solution)/shard_map/reduce_sum | solution.py:279
  1.5 0.6 and_convert_fusion.keep
  2.1 0.6 subtract_clamp_fusion.pick
  2.7 0.2 fusion.1
  2.8 0.7 copy.8.local_keep
  3.5 0.3 fusion
  3.9 0.7 copy.7.local_pick
  4.5 0.0 copy-start
  4.5 75.3 %inversion_step.1 = (f32[2,2,1536,128]{3,2,1,0:T(8,128)}, f32[1024,128]{1,0:T(8,128)}) custom-call(s32[2,16]{1,0:T(2,128)} %subtract_clamp_fusion.pick, f32[2,16]{1,0:T(2,128)} %and_convert_fusion.keep, s32[2,12]{1,0:T(2,128)} %copy.7.local_pick, f32[2,12]{1,0:T(2,128)} %copy.8.local_keep, bf16[2,2,2,128,128]{4,3,2,1,0:T(8,128)(2,1)} %bitcast.3, ...), custom_call_target="tpu_custom_call" | custom-call | tf_op jit(solution)/shard_map/inversion_step/pallas_call | solution.py:296
  79.8 0.0 copy-done
  79.8 1.9 %convert_subtract_fusion = f32[2,2,256,128]{3,2,1,0:T(8,128)} fusion(f32[2,2,256,128]{3,2,1,0:T(8,128)} %bitcast.2, bf16[2,2,256,128]{3,2,1,0:T(8,128)(2,1)S(1)} %copy-done), kind=kLoop, calls=%fused_computation | loop fusion | flops 262144 | bytes 1310720 | tf_op jit(solution)/shard_map/sub | solution.py:317
  81.7 3.8 %copy.10 = f32[2,2,1536,128]{3,2,1,0:T(8,128)} copy(f32[2,2,1536,128]{3,2,1,0:T(8,128)} %get-tuple-element.8) | data formatting | bytes 6291456
  (1 shorter events, 0.0 us)
Async XLA Ops:
  4.5 75.3 %copy-start = (bf16[2,2,256,128]{3,2,1,0:T(8,128)(2,1)S(1)}, bf16[2,2,256,128]{3,2,1,0:T(8,128)(2,1)}, u32[]{:S(2)}) copy-start(bf16[2,2,256,128]{3,2,1,0:T(8,128)(2,1)} %param.7) | copy-start | bytes 786436
where the time goes:
time: 86.5 us; the launch traced here: 85.5 us
  Pallas kernels  75.3 us (87%)
  local copies, waits for them, and re-layouts  5.12 us (6%)
  other arithmetic  4.42 us (5%)
    pallas_call x1, Pallas kernels, local(): pl.pallas_call(functools.partial(kernel, n, ny), out_shape=(jax.ShapeDtyp...  75.3 us
    unnamed x3, local copies, waits for them, and re-layouts  3.76 us
    sub x1, other arithmetic, local(): diag_blocks.astype(jnp.float32) - correction.reshape(diag_blocks.shape)  1.9 us

commit v1 on v0

v1 whole, which is shorter than its diff:
```python
import functools

import jax
import jax.numpy as jnp
from jax import lax
from jax.experimental import pallas as pl
from jax.experimental.pallas import tpu as pltpu
from jax.sharding import PartitionSpec as P

NSN = 2
BLK = 128
MESH = pl.DeviceIdType.MESH
ANY = pl.BlockSpec(memory_space=pl.ANY)
VMEM = pl.BlockSpec(memory_space=pltpu.VMEM)
SMEM = pl.BlockSpec(memory_space=pltpu.SMEM)


def aligned(start, size):
    return pl.ds(pl.multiple_of(start, size), size)


def index_tables(lists_s, order_s, lists_v, order_v, pick, keep, local_pick, local_keep, first, row, blocks_col, blocks_row):
    order = order_v[...]
    storage = lax.broadcasted_iota(jnp.int32, order.shape, 1)
    for k in range(lists_s.shape[0]):
        for j in range(lists_s.shape[1]):
            at = jnp.sum(jnp.where(order == lists_s[k, j], storage, 0)) - first
            inside = (at >= 0) & (at < blocks_col)
            pick[k, j] = jnp.clip(at, 0, blocks_col - 1)
            keep[k, j] = jnp.where(inside, 1.0, 0.0)
        listed = lists_v[k:k + 1, :]
        entry = lax.broadcasted_iota(jnp.int32, listed.shape, 1) + 1
        for t in range(blocks_row):
            found = jnp.sum(jnp.where(listed == order_s[0, row * blocks_row + t], entry, 0))
            local_pick[k, t] = jnp.clip(found - 1, 0, lists_s.shape[1] - 1)
            local_keep[k, t] = jnp.where(found > 0, 1.0, 0.0)


def kernel(n, ny, lists_s, order_s, lists_v, order_v, x_ref, a_ref, diag_ref, out_ref, sum_ref,
           pick, keep, local_pick, local_keep, a_buf, g_ref, own, oth, recv, bbuf, mine, parts, diag,
           a_sem, loc_sem, diag_sem, z_send, z_recv, y_send, y_recv, s_send, s_recv,
           v_send, v_recv, o_sem, r_send, r_recv, b_send, b_recv):
    nz = n // ny
    span = g_ref.shape[3] * BLK // n
    rows = a_ref.shape[1]
    blocks_col = a_ref.shape[2] // BLK
    blocks_row = rows // BLK
    tile = rows if rows <= 1536 else BLK
    per = max(1, span // BLK)
    unit = min(span, BLK)
    row = lax.axis_index("row")
    col = lax.axis_index("col")
    z = row // ny
    y = row % ny
    oy = ny - 1 - y
    sibling = {"col": 1 - col}
    up = {"row": row + ny}
    down = {"row": row - ny}
    across = {"row": z * ny + oy}
    size = sum_ref.shape[0] // (NSN * n)

    def place(k, r):
        return aligned(k * n * size + r * size, size)

    def stream(b):
        return pltpu.make_async_copy(a_ref.at[:, :, aligned(b * BLK, BLK)], a_buf.at[b], a_sem.at[b])

    def start_stream(b, carry):
        stream(b).start()
        return carry

    def wait_stream(b, carry):
        stream(b).wait()
        return carry

    def slot(c, k, r):
        if span >= BLK:
            return g_ref.at[c, k, :, pl.ds(r * per, per)]
        return g_ref.at[c, k, :, r * span // BLK, aligned(r * span % BLK, span)]

    def local(k):
        return pltpu.make_async_copy(x_ref.at[k], slot(col, k, row), loc_sem.at[k])

    def own_diag(k):
        return pltpu.make_async_copy(diag_ref.at[place(k, row)], diag.at[k], diag_sem.at[k])

    for k in range(NSN):
        local(k).start()
    lax.fori_loop(0, blocks_col, start_stream, 0)

    barrier = pltpu.get_barrier_semaphore()
    pl.semaphore_signal(barrier, inc=1, device_id=sibling, device_id_type=MESH)
    for d in range(1, n):
        pl.semaphore_signal(barrier, inc=1, device_id={"row": (row + d) % n}, device_id_type=MESH)
    pl.semaphore_wait(barrier, n)

    def copy(src, c, k, r, send, got, target):
        return pltpu.make_async_remote_copy(
            src_ref=src, dst_ref=slot(c, k, r), send_sem=send, recv_sem=got,
            device_id=target, device_id_type=MESH)

    def line(src, k, zz, target):
        return copy(src, col, k, zz * ny + y, z_send.at[k, zz], z_recv.at[k, zz], target)

    def side(src, k, zz, yy):
        return copy(src, col, k, zz * ny + yy, y_send.at[k, zz], y_recv.at[k, zz], across)

    def sib(src, c, k, r):
        return copy(src, c, k, r, s_send.at[k, r], s_recv.at[k, r], sibling)

    def here(k, zz, yy):
        return slot(col, k, zz * ny + yy)

    def first_up(k):
        return copy(x_ref.at[k], col, k, row, z_send.at[k, nz], z_recv.at[k, z], up)

    def first_down(k):
        return copy(x_ref.at[k], col, k, row, z_send.at[k, nz + 1], z_recv.at[k, z], down)

    for k in range(NSN):
        side(x_ref.at[k], k, z, y).start()
        pl.when(z < nz - 1)(lambda k=k: first_up(k).start())
        pl.when(z > 0)(lambda k=k: first_down(k).start())
        sib(x_ref.at[k], col, k, row).start()
    for k in range(NSN):
        own_diag(k).start()
    index_tables(lists_s, order_s, lists_v, order_v, pick, keep, local_pick, local_keep,
                 col * blocks_col, row, blocks_col, blocks_row)
    own[...] = jnp.zeros_like(own)
    oth[...] = jnp.zeros_like(oth)
    mine[...] = jnp.zeros_like(mine)
    for k in range(NSN):
        local(k).wait()

    def from_line(k, zz, forward, target):
        line(here(k, zz, y), k, zz, target).wait_recv()

        @pl.when(forward)
        def _():
            line(here(k, zz, y), k, zz, target).start()

        side(here(k, zz, y), k, zz, y).start()
        sib(here(k, zz, y), col, k, zz * ny + y).start()

    def from_side(k, zz):
        side(here(k, zz, oy), k, zz, oy).wait_recv()
        sib(here(k, zz, oy), col, k, zz * ny + oy).start()

    outs = (own, oth)

    def multiply(k, r):
        sib(slot(1 - col, k, r), 1 - col, k, r).wait_recv()
        if unit < BLK:
            bbuf[...] = jnp.zeros_like(bbuf)
        for e in range(per):
            start = r * span + e * BLK
            scale = keep[k, start // BLK]
            base = e * 2 * BLK
            if unit < BLK:
                shift = start % BLK
                top = aligned(base + shift, unit)
                low = aligned(base + BLK + shift, unit)
            else:
                top = pl.ds(base, unit)
                low = pl.ds(base + BLK, unit)
            for rel in range(2):
                c = col if rel == 0 else 1 - col
                at = pl.ds(0, unit) if unit == BLK else aligned(start % BLK, unit)
                real = (g_ref[c, k, 0, start // BLK, at, :].astype(jnp.float32) * scale).astype(jnp.bfloat16)
                imag = (g_ref[c, k, 1, start // BLK, at, :].astype(jnp.float32) * scale).astype(jnp.bfloat16)
                left = rel * 2 * BLK
                bbuf[top, left:left + BLK] = -real
                bbuf[top, left + BLK:left + 2 * BLK] = -imag
                bbuf[low, left:left + BLK] = imag
                bbuf[low, left + BLK:left + 2 * BLK] = -real

        def by_tile(t, inner):
            at = aligned(t * tile, tile)
            pieces = []
            for e in range(per):
                block = pick[k, (r * span + e * BLK) // BLK]
                pieces += [a_buf[block, 0, at, :], a_buf[block, 1, at, :]]
            left = jnp.concatenate(pieces, axis=1)
            for rel in range(2):
                found = jnp.dot(left, bbuf[:, rel * 2 * BLK:(rel + 1) * 2 * BLK],
                                preferred_element_type=jnp.float32)
                outs[rel][k, 0, at, :] += found[:, :BLK]
                outs[rel][k, 1, at, :] += found[:, BLK:]
            return inner

        lax.fori_loop(0, rows // tile, by_tile, 0)

    def swap(k):
        return pltpu.make_async_remote_copy(
            src_ref=oth.at[k], dst_ref=recv.at[k], send_sem=v_send.at[k], recv_sem=v_recv.at[k],
            device_id=sibling, device_id_type=MESH)

    steps = 2 * nz
    last = NSN + 4 * (steps - 1)

    def entry(e, carry):
        pl.when(e == last)(lambda: swap(0).start())
        g = (e - NSN) // 4
        q = (e - NSN) % 4
        away = g // 2 + 1 - q // 2
        mine_first = e < NSN
        k = jnp.where(mine_first, e, g % 2)
        zz = z + jnp.where(mine_first, 0, jnp.where(q % 2 == 0, -away, away))
        yy = jnp.where(mine_first | (q // 2 == 0), y, oy)
        valid = mine_first | ((zz >= 0) & (zz < nz) & ((away > 0) | (q % 2 == 0)))
        pl.when(valid)(lambda: multiply(k, zz * ny + yy))
        return carry

    def done_by(m):
        lag = jnp.where(m < 4, 2, jnp.where(m < steps - 1, 1, 0))
        return jnp.where(m < 1, 0, NSN + 4 * jnp.maximum(m - lag + 1, 0))

    def step(m, carry):
        d = m // 2 + 1
        k = m % 2
        pl.when(z - d >= 0)(lambda: from_line(k, z - d, z < nz - 1, up))
        pl.when(z + d < nz)(lambda: from_line(k, z + d, z > 0, down))
        pl.when(z - d + 1 >= 0)(lambda: from_side(k, z - d + 1))
        pl.when((d > 1) & (z + d - 1 < nz))(lambda: from_side(k, z + d - 1))
        pl.when(m == 1)(lambda: lax.fori_loop(0, blocks_col, wait_stream, None))
        lax.fori_loop(done_by(m - 1), done_by(m), entry, 0)
        return carry

    lax.fori_loop(0, steps, step, 0)
    swap(1).start()

    def scatter(k, d):
        to = (row + d) % n
        return pltpu.make_async_remote_copy(
            src_ref=mine.at[place(k, to)], dst_ref=parts.at[k, d],
            send_sem=r_send.at[k, d], recv_sem=r_recv.at[k, d],
            device_id={"row": to}, device_id_type=MESH)

    def spread(k, d):
        return pltpu.make_async_remote_copy(
            src_ref=parts.at[k, 0], dst_ref=sum_ref.at[place(k, row)],
            send_sem=b_send.at[k, d], recv_sem=b_recv.at[k, d],
            device_id={"row": (row + d) % n}, device_id_type=MESH)

    group = 3 if blocks_row % 3 == 0 else 1
    width = 2 * BLK
    for k in range(NSN):
        swap(k).wait_recv()
        own[k] += recv[k]
        pltpu.make_async_copy(own.at[k], out_ref.at[k], o_sem.at[k]).start()

        def correct(s, carry, k=k):
            left, right = [], []
            for u in range(group):
                t = s * group + u
                j = local_pick[k, t]
                scale = local_keep[k, t]
                for p in range(2):
                    left.append(jnp.concatenate([g_ref[0, k, p, j], g_ref[1, k, p, j]], axis=1))
                real = own[k, 0, aligned(t * BLK, BLK), :] * scale
                imag = own[k, 1, aligned(t * BLK, BLK), :] * scale
                right.append(jnp.concatenate([real, imag], axis=1))
                right.append(jnp.concatenate([-imag, real], axis=1))
            factor = jnp.concatenate(left, axis=0)
            wide = jnp.concatenate(right, axis=0)
            total = None
            for _ in range(2):
                piece = wide.astype(jnp.bfloat16)
                wide = wide - piece.astype(jnp.float32)
                term = lax.dot_general(factor, piece, (((0,), (0,)), ((), ())),
                                       preferred_element_type=jnp.float32)
                total = term if total is None else total + term
            mine[2 * k * width:(2 * k + 1) * width, :] += total[:, :BLK]
            mine[(2 * k + 1) * width:(2 * k + 2) * width, :] += total[:, BLK:]
            return carry

        lax.fori_loop(0, blocks_row // group, correct, 0)
        for d in range(1, n):
            scatter(k, d).start()

    for k in range(NSN):
        own_diag(k).wait()
        total = mine[place(k, row), :]
        for d in range(1, n):
            scatter(k, d).wait_recv()
            total = total + parts[k, d]
        total = diag[k].astype(jnp.float32) - total
        parts[k, 0] = total
        sum_ref[place(k, row), :] = total
        for d in range(1, n):
            spread(k, d).start()

    for k in range(NSN):
        for r in range(n):
            sib(slot(col, k, r), col, k, r).wait_send()
        for zz in range(nz):
            side(here(k, zz, y), k, zz, y).wait_send()
            pl.when(((zz < z) & (z < nz - 1)) | ((zz > z) & (z > 0)))(
                lambda k=k, zz=zz: line(here(k, zz, y), k, zz, up).wait_send())
        pl.when(z < nz - 1)(lambda k=k: first_up(k).wait_send())
        pl.when(z > 0)(lambda k=k: first_down(k).wait_send())
        swap(k).wait_send()
        pltpu.make_async_copy(own.at[k], out_ref.at[k], o_sem.at[k]).wait()
        for d in range(1, n):
            scatter(k, d).wait_send()
            spread(k, d).wait()


def local(n, inverse_pairs, factor_rows, diag_blocks, row_lists, block_order):
    rows, cols = inverse_pairs.shape[1:]
    blocks_row, blocks_col = rows // BLK, cols // BLK
    listed = row_lists.shape[1]
    order = block_order.reshape(1, -1)

    ny = 2 if n % 2 == 0 else 1
    nz = n // ny
    span, half = factor_rows.shape[2:]
    size = NSN * 2 * 2 * half
    per = max(1, span // BLK)
    shards = factor_rows.reshape(NSN, 2, per, BLK, half) if span >= BLK else factor_rows
    dma = pltpu.SemaphoreType.DMA
    side = (NSN, 2, rows, half)
    values, schur = pl.pallas_call(
        functools.partial(kernel, n, ny),
        out_shape=(jax.ShapeDtypeStruct(side, jnp.float32), jax.ShapeDtypeStruct((size, half), jnp.float32)),
        in_specs=[SMEM, SMEM, VMEM, VMEM, ANY, ANY, ANY],
        out_specs=(ANY, VMEM),
        scratch_shapes=[
            pltpu.SMEM((NSN, listed), jnp.int32),
            pltpu.SMEM((NSN, listed), jnp.float32),
            pltpu.SMEM((NSN, blocks_row), jnp.int32),
            pltpu.SMEM((NSN, blocks_row), jnp.float32),
            pltpu.VMEM((blocks_col, 2, rows, BLK), jnp.bfloat16),
            pltpu.VMEM((2, NSN, 2, listed, BLK, half), jnp.bfloat16),
            pltpu.VMEM(side, jnp.float32),
            pltpu.VMEM(side, jnp.float32),
            pltpu.VMEM(side, jnp.float32),
            pltpu.VMEM((per * 2 * BLK, 4 * BLK), jnp.bfloat16),
            pltpu.VMEM((size, half), jnp.float32),
            pltpu.VMEM((NSN, n, size // (NSN * n), half), jnp.float32),
            pltpu.VMEM((NSN, size // (NSN * n), half), jnp.bfloat16),
            dma((blocks_col,)), dma((NSN,)), dma((NSN,)), dma((NSN, nz + 2)), dma((NSN, nz)),
            dma((NSN, nz)), dma((NSN, nz)), dma((NSN, n)), dma((NSN, n)),
            dma((NSN,)), dma((NSN,)), dma((NSN,)), dma((NSN, n)), dma((NSN, n)), dma((NSN, n)), dma((NSN, n)),
        ],
        compiler_params=pltpu.CompilerParams(
            collective_id=0, has_side_effects=True, vmem_limit_bytes=66000000),
        name="inversion_step",
    )(row_lists, order, row_lists, order, shards, inverse_pairs, diag_blocks.reshape(size, half))
    return (values, schur.reshape(diag_blocks.shape))


def solution(mesh):
    in_specs = (
        P("pole", "row", "col"),
        P("pole", None, "row", "col"),
        P("pole", None, None, "col"),
        P(),
        P(),
    )
    out_specs = (P("pole", None, "row", "col"), P("pole", None, None, "col"))
    return jax.shard_map(functools.partial(local, mesh.shape["row"]), mesh=mesh, in_specs=in_specs,
                         out_specs=out_specs, check_vma=False)
```

time: 86.5 us -> 72.6 us (0.84); the launches traced: 85.5 us -> 72.5 us
  Pallas kernels: 75.3 us -> 67.2 us
  other arithmetic: 4.42 us -> 0 us
    pallas_call x1, Pallas kernels: 75.3 us -> 67.2 us  [local(): pl.pallas_call(functools.partial(kernel, n, ny), out_shape=(jax.ShapeDtyp...]
    sub x1 -> x0, other arithmetic: 1.9 us -> none  [local(): diag_blocks.astype(jnp.float32) - correction.reshape(diag_blocks.shape)]
    reduce_sum x3 -> x0, other arithmetic: 1.38 us -> none  [the longest x1 0.88 us: local(): position = jnp.sum(jnp.where(hits, storage, 0), axis=2).astype(jnp.int32)]
    reduce_sum x2 -> x0, local copies, waits for them, and re-layouts: 1.36 us -> none  [the longest x1 0.68 us: local(): local_keep = jnp.sum(found.astype(jnp.float32), axis=2)]
    unnamed x3 -> x4, local copies, waits for them, and re-layouts: 3.76 us -> 4.61 us
where the time goes in v1:
time: 72.6 us; the launch traced here: 72.5 us
  Pallas kernels  67.2 us (93%)
  local copies, waits for them, and re-layouts  4.61 us (6%)
    pallas_call x1, Pallas kernels, local(): pl.pallas_call(functools.partial(kernel, n, ny), out_shape=(jax.ShapeDtyp...  67.2 us
    unnamed x4, local copies, waits for them, and re-layouts  4.61 us

profile of v1, /device:TPU:0, one launch (start us, length us, event | category | flops | bytes accessed | tf_op | source)
XLA Modules:
  0.0 72.5 jit_solution(9886351695836795401)
XLA Ops:
  0.6 67.2 %inversion_step.1 = (f32[2,2,1536,128]{3,2,1,0:T(8,128)}, f32[1024,128]{1,0:T(8,128)}) custom-call(s32[2,16]{1,0:T(2,128)} %lists_v.1, s32[1,96]{1,0:T(1,128)} %bitcast.7, s32[2,16]{1,0:T(2,128)} %lists_v.1, s32[1,96]{1,0:T(1,128)} %bitcast.8, bf16[2,2,2,128,128]{4,3,2,1,0:T(8,128)(2,1)} %bitcast.5, bf16[2,1536,6144]{2,1,0:T(8,128)(2,1)} %a_ref.1, ...), custom_call_target="tpu_custom_call" | custom-call | tf_op jit(solution)/shard_map/inversion_step/pallas_call | solution.py:323
  67.8 0.0 copy-start
  67.8 3.8 %copy.9 = f32[2,2,1536,128]{3,2,1,0:T(8,128)} copy(f32[2,2,1536,128]{3,2,1,0:T(8,128)} %get-tuple-element.8) | data formatting | bytes 6291456
  71.7 0.0 copy-done
  71.7 0.8 %copy.10 = f32[2,2,256,128]{3,2,1,0:T(8,128)} copy(f32[2,2,256,128]{3,2,1,0:T(8,128)S(1)} %bitcast.4) | data formatting | bytes 1048576
Async XLA Ops:
  67.8 3.8 %copy-start = (f32[1024,128]{1,0:T(8,128)S(1)}, f32[1024,128]{1,0:T(8,128)}, u32[]{:S(2)}) copy-start(f32[1024,128]{1,0:T(8,128)} %get-tuple-element.5) | copy-start | bytes 1572868

commit v2 on v1

--- a/solution.py
+++ b/solution.py
@@ -36,10 +36,19 @@
             local_keep[k, t] = jnp.where(found > 0, 1.0, 0.0)
 
 
+def coded(value):
+    most = jnp.maximum(jnp.max(jnp.abs(value), axis=0, keepdims=True), 1e-33)
+    return jnp.round(value * (32767.0 / most)).astype(jnp.int32).astype(jnp.int16), most * (1.0 / 32767.0)
+
+
+def decoded(code, scale):
+    return code.astype(jnp.int32).astype(jnp.float32) * scale
+
+
 def kernel(n, ny, lists_s, order_s, lists_v, order_v, x_ref, a_ref, diag_ref, out_ref, sum_ref,
-           pick, keep, local_pick, local_keep, a_buf, g_ref, own, oth, recv, bbuf, mine, parts, diag,
+           pick, keep, local_pick, local_keep, a_buf, g_ref, own, oth, recv, bbuf, mine, codes, scales, got_codes, got_scales, all_codes, all_scales, diag,
            a_sem, loc_sem, diag_sem, z_send, z_recv, y_send, y_recv, s_send, s_recv,
-           v_send, v_recv, o_sem, r_send, r_recv, b_send, b_recv):
+           v_send, v_recv, o_sem, r_send, r_recv, rs_send, rs_recv, b_send, b_recv, bs_send, bs_recv):
     nz = n // ny
     span = g_ref.shape[3] * BLK // n
     rows = a_ref.shape[1]
@@ -190,16 +199,32 @@
 
         lax.fori_loop(0, rows // tile, by_tile, 0)
 
-    def swap(k):
+    group = 3 if blocks_row % 3 == 0 else 1
+    strips = blocks_row // group
+    high = group * BLK
+
+    def strip(k, s):
+        return k, slice(None), aligned(s * high, high)
+
+    def swap(k, s):
         return pltpu.make_async_remote_copy(
-            src_ref=oth.at[k], dst_ref=recv.at[k], send_sem=v_send.at[k], recv_sem=v_recv.at[k],
+            src_ref=oth.at[strip(k, s)], dst_ref=recv.at[strip(k, s)], send_sem=v_send.at[k, s], recv_sem=v_recv.at[k, s],
             device_id=sibling, device_id_type=MESH)
+
+    def start_swaps(k):
+        def one(s, carry):
+            swap(k, s).start()
+            return carry
+        lax.fori_loop(0, strips, one, 0)
+
+    def put(k, s):
+        return pltpu.make_async_copy(own.at[strip(k, s)], out_ref.at[strip(k, s)], o_sem.at[k, s])
 
     steps = 2 * nz
     last = NSN + 4 * (steps - 1)
 
     def entry(e, carry):
-        pl.when(e == last)(lambda: swap(0).start())
+        pl.when(e == last)(lambda: start_swaps(0))
         g = (e - NSN) // 4
         q = (e - NSN) % 4
         away = g // 2 + 1 - q // 2
@@ -212,7 +237,7 @@
         return carry
 
     def done_by(m):
-        lag = jnp.where(m < 4, 2, jnp.where(m < steps - 1, 1, 0))
+        lag = jnp.where(m >= steps - 2, 0, jnp.where(m < 4, 2, 1))
         return jnp.where(m < 1, 0, NSN + 4 * jnp.maximum(m - lag + 1, 0))
 
     def step(m, carry):
@@ -227,29 +252,38 @@
         return carry
 
     lax.fori_loop(0, steps, step, 0)
-    swap(1).start()
+    start_swaps(1)
 
     def scatter(k, d):
         to = (row + d) % n
-        return pltpu.make_async_remote_copy(
-            src_ref=mine.at[place(k, to)], dst_ref=parts.at[k, d],
+        code = pltpu.make_async_remote_copy(
+            src_ref=codes.at[k, to], dst_ref=got_codes.at[k, d],
             send_sem=r_send.at[k, d], recv_sem=r_recv.at[k, d],
             device_id={"row": to}, device_id_type=MESH)
-
-    def spread(k, d):
-        return pltpu.make_async_remote_copy(
-            src_ref=parts.at[k, 0], dst_ref=sum_ref.at[place(k, row)],
+        scale = pltpu.make_async_remote_copy(
+            src_ref=scales.at[k, to], dst_ref=got_scales.at[k, d],
+            send_sem=rs_send.at[k, d], recv_sem=rs_recv.at[k, d],
+            device_id={"row": to}, device_id_type=MESH)
+        return code, scale
+
+    def spread(k, d, owner):
+        to = (row + d) % n
+        code = pltpu.make_async_remote_copy(
+            src_ref=all_codes.at[k, owner], dst_ref=all_codes.at[k, owner],
             send_sem=b_send.at[k, d], recv_sem=b_recv.at[k, d],
-            device_id={"row": (row + d) % n}, device_id_type=MESH)
-
-    group = 3 if blocks_row % 3 == 0 else 1
+            device_id={"row": to}, device_id_type=MESH)
+        scale = pltpu.make_async_remote_copy(
+            src_ref=all_scales.at[k, owner], dst_ref=all_scales.at[k, owner],
+            send_sem=bs_send.at[k, d], recv_sem=bs_recv.at[k, d],
+            device_id={"row": to}, device_id_type=MESH)
+        return code, scale
+
     width = 2 * BLK
     for k in range(NSN):
-        swap(k).wait_recv()
-        own[k] += recv[k]
-        pltpu.make_async_copy(own.at[k], out_ref.at[k], o_sem.at[k]).start()
-
         def correct(s, carry, k=k):
+            swap(k, s).wait_recv()
+            own[strip(k, s)] += recv[strip(k, s)]
+            put(k, s).start()
             left, right = [], []
             for u in range(group):
                 t = s * group + u
@@ -274,21 +308,28 @@
             mine[(2 * k + 1) * width:(2 * k + 2) * width, :] += total[:, BLK:]
             return carry
 
-        lax.fori_loop(0, blocks_row // group, correct, 0)
+        lax.fori_loop(0, strips, correct, 0)
+
+        def encode(r, carry, k=k):
+            codes[k, r], scales[k, r] = coded(mine[place(k, r), :])
+            return carry
+
+        lax.fori_loop(0, n, encode, 0)
         for d in range(1, n):
-            scatter(k, d).start()
+            for c in scatter(k, d):
+                c.start()
 
     for k in range(NSN):
         own_diag(k).wait()
         total = mine[place(k, row), :]
         for d in range(1, n):
-            scatter(k, d).wait_recv()
-            total = total + parts[k, d]
-        total = diag[k].astype(jnp.float32) - total
-        parts[k, 0] = total
-        sum_ref[place(k, row), :] = total
+            for c in scatter(k, d):
+                c.wait_recv()
+            total = total + decoded(got_codes[k, d], got_scales[k, d])
+        all_codes[k, row], all_scales[k, row] = coded(diag[k].astype(jnp.float32) - total)
         for d in range(1, n):
-            spread(k, d).start()
+            for c in spread(k, d, row):
+                c.start()
 
     for k in range(NSN):
         for r in range(n):
@@ -299,11 +340,26 @@
                 lambda k=k, zz=zz: line(here(k, zz, y), k, zz, up).wait_send())
         pl.when(z < nz - 1)(lambda k=k: first_up(k).wait_send())
         pl.when(z > 0)(lambda k=k: first_down(k).wait_send())
-        swap(k).wait_send()
-        pltpu.make_async_copy(own.at[k], out_ref.at[k], o_sem.at[k]).wait()
+        def drain(s, carry, k=k):
+            swap(k, s).wait_send()
+            put(k, s).wait()
+            return carry
+
+        lax.fori_loop(0, strips, drain, 0)
         for d in range(1, n):
-            scatter(k, d).wait_send()
-            spread(k, d).wait()
+            for c in scatter(k, d) + spread(k, d, row):
+                c.wait_send()
+
+    for k in range(NSN):
+        for d in range(1, n):
+            for c in spread(k, d, (row - d) % n):
+                c.wait_recv()
+
+        def decode(r, carry, k=k):
+            sum_ref[place(k, r), :] = decoded(all_codes[k, r], all_scales[k, r])
+            return carry
+
+        lax.fori_loop(0, n, decode, 0)
 
 
 def local(n, inverse_pairs, factor_rows, diag_blocks, row_lists, block_order):
@@ -316,6 +372,7 @@
     nz = n // ny
     span, half = factor_rows.shape[2:]
     size = NSN * 2 * 2 * half
+    piece = size // (NSN * n)
     per = max(1, span // BLK)
     shards = factor_rows.reshape(NSN, 2, per, BLK, half) if span >= BLK else factor_rows
     dma = pltpu.SemaphoreType.DMA
@@ -337,11 +394,15 @@
             pltpu.VMEM(side, jnp.float32),
             pltpu.VMEM((per * 2 * BLK, 4 * BLK), jnp.bfloat16),
             pltpu.VMEM((size, half), jnp.float32),
-            pltpu.VMEM((NSN, n, size // (NSN * n), half), jnp.float32),
-            pltpu.VMEM((NSN, size // (NSN * n), half), jnp.bfloat16),
+            pltpu.VMEM((NSN, n, piece, half), jnp.int16), pltpu.VMEM((NSN, n, 1, half), jnp.float32),
+            pltpu.VMEM((NSN, n, piece, half), jnp.int16), pltpu.VMEM((NSN, n, 1, half), jnp.float32),
+            pltpu.VMEM((NSN, n, piece, half), jnp.int16), pltpu.VMEM((NSN, n, 1, half), jnp.float32),
+            pltpu.VMEM((NSN, piece, half), jnp.bfloat16),
             dma((blocks_col,)), dma((NSN,)), dma((NSN,)), dma((NSN, nz + 2)), dma((NSN, nz)),
             dma((NSN, nz)), dma((NSN, nz)), dma((NSN, n)), dma((NSN, n)),
-            dma((NSN,)), dma((NSN,)), dma((NSN,)), dma((NSN, n)), dma((NSN, n)), dma((NSN, n)), dma((NSN, n)),
+            dma((NSN, blocks_row)), dma((NSN, blocks_row)), dma((NSN, blocks_row)),
+            dma((NSN, n)), dma((NSN, n)), dma((NSN, n)), dma((NSN, n)),
+            dma((NSN, n)), dma((NSN, n)), dma((NSN, n)), dma((NSN, n)),
         ],
         compiler_params=pltpu.CompilerParams(
             collective_id=0, has_side_effects=True, vmem_limit_bytes=66000000),

time: 72.6 us -> 63.1 us (0.87)
  Pallas kernels: 67.2 us -> 57.7 us
    pallas_call x1, Pallas kernels: 67.2 us -> 57.7 us  [local(): pl.pallas_call(functools.partial(kernel, n, ny), out_shape=(jax.ShapeDtyp...]
where the time goes in v2:
time: 63.1 us; the launch traced here: 62.9 us
  Pallas kernels  57.7 us (91%)
  local copies, waits for them, and re-layouts  4.61 us (7%)
  between operations  0.65 us (1%)
    pallas_call x1, Pallas kernels, local(): pl.pallas_call(functools.partial(kernel, n, ny), out_shape=(jax.ShapeDtyp...  57.7 us
    unnamed x4, local copies, waits for them, and re-layouts  4.61 us

profile of v2, /device:TPU:0, one launch (start us, length us, event | category | flops | bytes accessed | tf_op | source)
XLA Modules:
  0.0 62.9 jit_solution(10332668150235377084)
XLA Ops:
  0.6 57.7 %inversion_step.1 = (f32[2,2,1536,128]{3,2,1,0:T(8,128)}, f32[1024,128]{1,0:T(8,128)}) custom-call(s32[2,16]{1,0:T(2,128)} %lists_v.1, s32[1,96]{1,0:T(1,128)} %bitcast.7, s32[2,16]{1,0:T(2,128)} %lists_v.1, s32[1,96]{1,0:T(1,128)} %bitcast.8, bf16[2,2,2,128,128]{4,3,2,1,0:T(8,128)(2,1)} %bitcast.5, bf16[2,1536,6144]{2,1,0:T(8,128)(2,1)} %a_ref.1, ...), custom_call_target="tpu_custom_call" | custom-call | tf_op jit(solution)/shard_map/inversion_step/pallas_call | solution.py:380
  58.3 0.0 copy-start
  58.3 3.8 %copy.9 = f32[2,2,1536,128]{3,2,1,0:T(8,128)} copy(f32[2,2,1536,128]{3,2,1,0:T(8,128)} %get-tuple-element.8) | data formatting | bytes 6291456
  62.1 0.0 copy-done
  62.1 0.8 %copy.10 = f32[2,2,256,128]{3,2,1,0:T(8,128)} copy(f32[2,2,256,128]{3,2,1,0:T(8,128)S(1)} %bitcast.4) | data formatting | bytes 1048576
Async XLA Ops:
  58.3 3.8 %copy-start = (f32[1024,128]{1,0:T(8,128)S(1)}, f32[1024,128]{1,0:T(8,128)}, u32[]{:S(2)}) copy-start(f32[1024,128]{1,0:T(8,128)} %get-tuple-element.5) | copy-start | bytes 1572868

commit v3 on v2

--- a/solution.py
+++ b/solution.py
@@ -45,8 +45,8 @@
     return code.astype(jnp.int32).astype(jnp.float32) * scale
 
 
-def kernel(n, ny, lists_s, order_s, lists_v, order_v, x_ref, a_ref, diag_ref, out_ref, sum_ref,
-           pick, keep, local_pick, local_keep, a_buf, g_ref, own, oth, recv, bbuf, mine, codes, scales, got_codes, got_scales, all_codes, all_scales, diag,
+def kernel(n, ny, lists_s, order_s, lists_v, order_v, x_ref, a_ref, diag_ref, own, sum_ref,
+           pick, keep, local_pick, local_keep, a_buf, g_ref, oth, recv, bbuf, mine, codes, scales, got_codes, got_scales, all_codes, all_scales, diag,
            a_sem, loc_sem, diag_sem, z_send, z_recv, y_send, y_recv, s_send, s_recv,
            v_send, v_recv, o_sem, r_send, r_recv, rs_send, rs_recv, b_send, b_recv, bs_send, bs_recv):
     nz = n // ny
@@ -217,8 +217,6 @@
             return carry
         lax.fori_loop(0, strips, one, 0)
 
-    def put(k, s):
-        return pltpu.make_async_copy(own.at[strip(k, s)], out_ref.at[strip(k, s)], o_sem.at[k, s])
 
     steps = 2 * nz
     last = NSN + 4 * (steps - 1)
@@ -283,7 +281,6 @@
         def correct(s, carry, k=k):
             swap(k, s).wait_recv()
             own[strip(k, s)] += recv[strip(k, s)]
-            put(k, s).start()
             left, right = [], []
             for u in range(group):
                 t = s * group + u
@@ -342,7 +339,6 @@
         pl.when(z > 0)(lambda k=k: first_down(k).wait_send())
         def drain(s, carry, k=k):
             swap(k, s).wait_send()
-            put(k, s).wait()
             return carry
 
         lax.fori_loop(0, strips, drain, 0)
@@ -379,9 +375,9 @@
     side = (NSN, 2, rows, half)
     values, schur = pl.pallas_call(
         functools.partial(kernel, n, ny),
-        out_shape=(jax.ShapeDtypeStruct(side, jnp.float32), jax.ShapeDtypeStruct((size, half), jnp.float32)),
+        out_shape=(pltpu.VMEM(side, jnp.float32), pltpu.VMEM((size, half), jnp.float32)),
         in_specs=[SMEM, SMEM, VMEM, VMEM, ANY, ANY, ANY],
-        out_specs=(ANY, VMEM),
+        out_specs=(VMEM, VMEM),
         scratch_shapes=[
             pltpu.SMEM((NSN, listed), jnp.int32),
             pltpu.SMEM((NSN, listed), jnp.float32),
@@ -389,7 +385,6 @@
             pltpu.SMEM((NSN, blocks_row), jnp.float32),
             pltpu.VMEM((blocks_col, 2, rows, BLK), jnp.bfloat16),
             pltpu.VMEM((2, NSN, 2, listed, BLK, half), jnp.bfloat16),
-            pltpu.VMEM(side, jnp.float32),
             pltpu.VMEM(side, jnp.float32),
             pltpu.VMEM(side, jnp.float32),
             pltpu.VMEM((per * 2 * BLK, 4 * BLK), jnp.bfloat16),
@@ -405,7 +400,7 @@
             dma((NSN, n)), dma((NSN, n)), dma((NSN, n)), dma((NSN, n)),
         ],
         compiler_params=pltpu.CompilerParams(
-            collective_id=0, has_side_effects=True, vmem_limit_bytes=66000000),
+            collective_id=0, has_side_effects=True, vmem_limit_bytes=58000000),
         name="inversion_step",
     )(row_lists, order, row_lists, order, shards, inverse_pairs, diag_blocks.reshape(size, half))
     return (values, schur.reshape(diag_blocks.shape))

time: 63.1 us -> 60.4 us (0.957)
  local copies, waits for them, and re-layouts: 4.61 us -> 2.46 us
    unnamed x4 -> x2, local copies, waits for them, and re-layouts: 4.61 us -> 2.46 us
where the time goes in v3:
time: 60.4 us; the launch traced here: 60.3 us
  Pallas kernels  57.2 us (95%)
  local copies, waits for them, and re-layouts  2.46 us (4%)
  between operations  0.64 us (1%)
    pallas_call x1, Pallas kernels, local(): pl.pallas_call(functools.partial(kernel, n, ny), out_shape=(pltpu.VMEM(si...  57.2 us
    unnamed x2, local copies, waits for them, and re-layouts  2.46 us

profile of v3, /device:TPU:0, one launch (start us, length us, event | category | flops | bytes accessed | tf_op | source)
XLA Modules:
  0.0 60.3 jit_solution(15095748344702700946)
XLA Ops:
  0.6 57.2 %inversion_step.1 = (f32[2,2,1536,128]{3,2,1,0:T(8,128)S(1)}, f32[1024,128]{1,0:T(8,128)S(1)}) custom-call(s32[2,16]{1,0:T(2,128)} %lists_v.1, s32[1,96]{1,0:T(1,128)} %bitcast.7, s32[2,16]{1,0:T(2,128)} %lists_v.1, s32[1,96]{1,0:T(1,128)} %bitcast.8, bf16[2,2,2,128,128]{4,3,2,1,0:T(8,128)(2,1)} %bitcast.5, bf16[2,1536,6144]{2,1,0:T(8,128)(2,1)} %a_ref.1, ...), custom_call_target="tpu_custom_call" | custom-call | tf_op jit(solution)/shard_map/inversion_step/pallas_call | solution.py:376
  57.8 1.7 %copy.9 = f32[2,2,1536,128]{3,2,1,0:T(8,128)} copy(f32[2,2,1536,128]{3,2,1,0:T(8,128)S(1)} %get-tuple-element.6) | data formatting | bytes 6291456
  59.5 0.8 %copy.10 = f32[2,2,256,128]{3,2,1,0:T(8,128)} copy(f32[2,2,256,128]{3,2,1,0:T(8,128)S(1)} %bitcast.4) | data formatting | bytes 1048576

commit v4 on v3

--- a/solution.py
+++ b/solution.py
@@ -37,7 +37,7 @@
 
 
 def coded(value):
-    most = jnp.maximum(jnp.max(jnp.abs(value), axis=0, keepdims=True), 1e-33)
+    most = jnp.maximum(jnp.max(jnp.abs(value), axis=-2, keepdims=True), 1e-33)
     return jnp.round(value * (32767.0 / most)).astype(jnp.int32).astype(jnp.int16), most * (1.0 / 32767.0)
 
 
@@ -46,7 +46,7 @@
 
 
 def kernel(n, ny, lists_s, order_s, lists_v, order_v, x_ref, a_ref, diag_ref, own, sum_ref,
-           pick, keep, local_pick, local_keep, a_buf, g_ref, oth, recv, bbuf, mine, codes, scales, got_codes, got_scales, all_codes, all_scales, diag,
+           pick, keep, local_pick, local_keep, a_top, a_low, g_ref, oth, recv, bbuf, mine, codes, scales, got_codes, got_scales, all_codes, all_scales, diag,
            a_sem, loc_sem, diag_sem, z_send, z_recv, y_send, y_recv, s_send, s_recv,
            v_send, v_recv, o_sem, r_send, r_recv, rs_send, rs_recv, b_send, b_recv, bs_send, bs_recv):
     nz = n // ny
@@ -54,7 +54,7 @@
     rows = a_ref.shape[1]
     blocks_col = a_ref.shape[2] // BLK
     blocks_row = rows // BLK
-    tile = rows if rows <= 1536 else BLK
+    tall = a_top.shape[2]
     per = max(1, span // BLK)
     unit = min(span, BLK)
     row = lax.axis_index("row")
@@ -71,16 +71,22 @@
     def place(k, r):
         return aligned(k * n * size + r * size, size)
 
-    def stream(b):
-        return pltpu.make_async_copy(a_ref.at[:, :, aligned(b * BLK, BLK)], a_buf.at[b], a_sem.at[b])
-
-    def start_stream(b, carry):
-        stream(b).start()
-        return carry
-
-    def wait_stream(b, carry):
-        stream(b).wait()
-        return carry
+    def stream(half, b):
+        a_half = a_low if half else a_top
+        return pltpu.make_async_copy(
+            a_ref.at[:, half * tall:(half + 1) * tall, aligned(b * BLK, BLK)], a_half.at[b], a_sem.at[half, b])
+
+    def start_stream(half):
+        def one(b, carry):
+            stream(half, b).start()
+            return carry
+        lax.fori_loop(0, blocks_col, one, 0)
+
+    def wait_stream(half):
+        def one(b, carry):
+            stream(half, b).wait()
+            return carry
+        lax.fori_loop(0, blocks_col, one, 0)
 
     def slot(c, k, r):
         if span >= BLK:
@@ -95,13 +101,15 @@
 
     for k in range(NSN):
         local(k).start()
-    lax.fori_loop(0, blocks_col, start_stream, 0)
+    for half in range(2):
+        start_stream(half)
 
     barrier = pltpu.get_barrier_semaphore()
     pl.semaphore_signal(barrier, inc=1, device_id=sibling, device_id_type=MESH)
-    for d in range(1, n):
-        pl.semaphore_signal(barrier, inc=1, device_id={"row": (row + d) % n}, device_id_type=MESH)
-    pl.semaphore_wait(barrier, n)
+    pl.semaphore_signal(barrier, inc=1, device_id=across, device_id_type=MESH)
+    pl.when(z < nz - 1)(lambda: pl.semaphore_signal(barrier, inc=1, device_id=up, device_id_type=MESH))
+    pl.when(z > 0)(lambda: pl.semaphore_signal(barrier, inc=1, device_id=down, device_id_type=MESH))
+    pl.semaphore_wait(barrier, 2 + jnp.where(z < nz - 1, 1, 0) + jnp.where(z > 0, 1, 0))
 
     def copy(src, c, k, r, send, got, target):
         return pltpu.make_async_remote_copy(
@@ -157,8 +165,9 @@
 
     outs = (own, oth)
 
-    def multiply(k, r):
-        sib(slot(1 - col, k, r), 1 - col, k, r).wait_recv()
+    def multiply(k, r, halves, fresh):
+        if fresh:
+            sib(slot(1 - col, k, r), 1 - col, k, r).wait_recv()
         if unit < BLK:
             bbuf[...] = jnp.zeros_like(bbuf)
         for e in range(per):
@@ -183,21 +192,21 @@
                 bbuf[low, left:left + BLK] = imag
                 bbuf[low, left + BLK:left + 2 * BLK] = -real
 
-        def by_tile(t, inner):
-            at = aligned(t * tile, tile)
+        at = slice(halves[0] * tall, (halves[-1] + 1) * tall)
+        left = []
+        for half in halves:
+            a_half = a_low if half else a_top
             pieces = []
             for e in range(per):
                 block = pick[k, (r * span + e * BLK) // BLK]
-                pieces += [a_buf[block, 0, at, :], a_buf[block, 1, at, :]]
-            left = jnp.concatenate(pieces, axis=1)
-            for rel in range(2):
-                found = jnp.dot(left, bbuf[:, rel * 2 * BLK:(rel + 1) * 2 * BLK],
-                                preferred_element_type=jnp.float32)
-                outs[rel][k, 0, at, :] += found[:, :BLK]
-                outs[rel][k, 1, at, :] += found[:, BLK:]
-            return inner
-
-        lax.fori_loop(0, rows // tile, by_tile, 0)
+                pieces += [a_half[block, 0], a_half[block, 1]]
+            left.append(jnp.concatenate(pieces, axis=1))
+        left = jnp.concatenate(left, axis=0) if len(left) > 1 else left[0]
+        for rel in range(2):
+            found = jnp.dot(left, bbuf[:, rel * 2 * BLK:(rel + 1) * 2 * BLK],
+                            preferred_element_type=jnp.float32)
+            outs[rel][k, 0, at, :] += found[:, :BLK]
+            outs[rel][k, 1, at, :] += found[:, BLK:]
 
     group = 3 if blocks_row % 3 == 0 else 1
     strips = blocks_row // group
@@ -218,25 +227,29 @@
         lax.fori_loop(0, strips, one, 0)
 
 
-    steps = 2 * nz
+    steps = max(2 * nz, 4)
     last = NSN + 4 * (steps - 1)
 
-    def entry(e, carry):
-        pl.when(e == last)(lambda: start_swaps(0))
-        g = (e - NSN) // 4
-        q = (e - NSN) % 4
-        away = g // 2 + 1 - q // 2
-        mine_first = e < NSN
-        k = jnp.where(mine_first, e, g % 2)
-        zz = z + jnp.where(mine_first, 0, jnp.where(q % 2 == 0, -away, away))
-        yy = jnp.where(mine_first | (q // 2 == 0), y, oy)
-        valid = mine_first | ((zz >= 0) & (zz < nz) & ((away > 0) | (q % 2 == 0)))
-        pl.when(valid)(lambda: multiply(k, zz * ny + yy))
-        return carry
+    def entries(low, high, halves, fresh):
+        def entry(e, carry):
+            if len(halves) > 1:
+                pl.when(e == last)(lambda: start_swaps(0))
+            g = (e - NSN) // 4
+            q = (e - NSN) % 4
+            away = g // 2 + 1 - q // 2
+            mine_first = e < NSN
+            k = jnp.where(mine_first, e, g % 2)
+            zz = z + jnp.where(mine_first, 0, jnp.where(q % 2 == 0, -away, away))
+            yy = jnp.where(mine_first | (q // 2 == 0), y, oy)
+            valid = mine_first | ((zz >= 0) & (zz < nz) & ((away > 0) | (q % 2 == 0)))
+            pl.when(valid)(lambda: multiply(k, zz * ny + yy, halves, fresh))
+            return carry
+
+        lax.fori_loop(low, high, entry, 0)
 
     def done_by(m):
-        lag = jnp.where(m >= steps - 2, 0, jnp.where(m < 4, 2, 1))
-        return jnp.where(m < 1, 0, NSN + 4 * jnp.maximum(m - lag + 1, 0))
+        ahead = NSN + 4 * jnp.where(m >= steps - 2, m + 1, m)
+        return jnp.where(m < 3, NSN + 8, NSN + 4 * jnp.where(m >= steps - 1, m + 1, m))
 
     def step(m, carry):
         d = m // 2 + 1
@@ -245,8 +258,13 @@
         pl.when(z + d < nz)(lambda: from_line(k, z + d, z > 0, down))
         pl.when(z - d + 1 >= 0)(lambda: from_side(k, z - d + 1))
         pl.when((d > 1) & (z + d - 1 < nz))(lambda: from_side(k, z + d - 1))
-        pl.when(m == 1)(lambda: lax.fori_loop(0, blocks_col, wait_stream, None))
-        lax.fori_loop(done_by(m - 1), done_by(m), entry, 0)
+        pl.when(m == 0)(lambda: wait_stream(0))
+        pl.when(m == 2)(lambda: wait_stream(1))
+        cut = NSN + 4
+        low, high = jnp.where(m % 2 == 0, 0, cut), jnp.where(m % 2 == 0, cut, cut + 4)
+        pl.when(m < 2)(lambda: entries(low, high, (0,), True))
+        pl.when((m >= 2) & (m < 4))(lambda: entries(low, high, (1,), False))
+        entries(done_by(m - 1), done_by(m), (0, 1), True)
         return carry
 
     lax.fori_loop(0, steps, step, 0)
@@ -307,11 +325,7 @@
 
         lax.fori_loop(0, strips, correct, 0)
 
-        def encode(r, carry, k=k):
-            codes[k, r], scales[k, r] = coded(mine[place(k, r), :])
-            return carry
-
-        lax.fori_loop(0, n, encode, 0)
+        codes[k], scales[k] = coded(mine[k * n * size:(k + 1) * n * size, :].reshape(codes.shape[1:]))
         for d in range(1, n):
             for c in scatter(k, d):
                 c.start()
@@ -351,11 +365,7 @@
             for c in spread(k, d, (row - d) % n):
                 c.wait_recv()
 
-        def decode(r, carry, k=k):
-            sum_ref[place(k, r), :] = decoded(all_codes[k, r], all_scales[k, r])
-            return carry
-
-        lax.fori_loop(0, n, decode, 0)
+        sum_ref[k * n * size:(k + 1) * n * size, :] = decoded(all_codes[k], all_scales[k]).reshape(n * size, sum_ref.shape[1])
 
 
 def local(n, inverse_pairs, factor_rows, diag_blocks, row_lists, block_order):
@@ -383,7 +393,8 @@
             pltpu.SMEM((NSN, listed), jnp.float32),
             pltpu.SMEM((NSN, blocks_row), jnp.int32),
             pltpu.SMEM((NSN, blocks_row), jnp.float32),
-            pltpu.VMEM((blocks_col, 2, rows, BLK), jnp.bfloat16),
+            pltpu.VMEM((blocks_col, 2, rows // 2, BLK), jnp.bfloat16),
+            pltpu.VMEM((blocks_col, 2, rows // 2, BLK), jnp.bfloat16),
             pltpu.VMEM((2, NSN, 2, listed, BLK, half), jnp.bfloat16),
             pltpu.VMEM(side, jnp.float32),
             pltpu.VMEM(side, jnp.float32),
@@ -393,7 +404,7 @@
             pltpu.VMEM((NSN, n, piece, half), jnp.int16), pltpu.VMEM((NSN, n, 1, half), jnp.float32),
             pltpu.VMEM((NSN, n, piece, half), jnp.int16), pltpu.VMEM((NSN, n, 1, half), jnp.float32),
             pltpu.VMEM((NSN, piece, half), jnp.bfloat16),
-            dma((blocks_col,)), dma((NSN,)), dma((NSN,)), dma((NSN, nz + 2)), dma((NSN, nz)),
+            dma((2, blocks_col)), dma((NSN,)), dma((NSN,)), dma((NSN, nz + 2)), dma((NSN, nz)),
             dma((NSN, nz)), dma((NSN, nz)), dma((NSN, n)), dma((NSN, n)),
             dma((NSN, blocks_row)), dma((NSN, blocks_row)), dma((NSN, blocks_row)),
             dma((NSN, n)), dma((NSN, n)), dma((NSN, n)), dma((NSN, n)),

time: 60.4 us -> 59.6 us (0.987)
  Pallas kernels: 57.2 us -> 56.4 us
    pallas_call x1, Pallas kernels: 57.2 us -> 56.4 us  [local(): pl.pallas_call(functools.partial(kernel, n, ny), out_shape=(pltpu.VMEM(si...]
where the time goes in v4:
time: 59.6 us; the launch traced here: 59.5 us
  Pallas kernels  56.4 us (95%)
  local copies, waits for them, and re-layouts  2.46 us (4%)
  between operations  0.64 us (1%)
    pallas_call x1, Pallas kernels, local(): pl.pallas_call(functools.partial(kernel, n, ny), out_shape=(pltpu.VMEM(si...  56.4 us
    unnamed x2, local copies, waits for them, and re-layouts  2.46 us

profile of v4, /device:TPU:0, one launch (start us, length us, event | category | flops | bytes accessed | tf_op | source)
XLA Modules:
  0.0 59.5 jit_solution(3369612698306060190)
XLA Ops:
  0.6 56.4 %inversion_step.1 = (f32[2,2,1536,128]{3,2,1,0:T(8,128)S(1)}, f32[1024,128]{1,0:T(8,128)S(1)}) custom-call(s32[2,16]{1,0:T(2,128)} %lists_v.1, s32[1,96]{1,0:T(1,128)} %bitcast.7, s32[2,16]{1,0:T(2,128)} %lists_v.1, s32[1,96]{1,0:T(1,128)} %bitcast.8, bf16[2,2,2,128,128]{4,3,2,1,0:T(8,128)(2,1)} %bitcast.5, bf16[2,1536,6144]{2,1,0:T(8,128)(2,1)} %a_ref.1, ...), custom_call_target="tpu_custom_call" | custom-call | tf_op jit(solution)/shard_map/inversion_step/pallas_call | solution.py:386
  57.0 1.7 %copy.9 = f32[2,2,1536,128]{3,2,1,0:T(8,128)} copy(f32[2,2,1536,128]{3,2,1,0:T(8,128)S(1)} %get-tuple-element.6) | data formatting | bytes 6291456
  58.7 0.8 %copy.10 = f32[2,2,256,128]{3,2,1,0:T(8,128)} copy(f32[2,2,256,128]{3,2,1,0:T(8,128)S(1)} %bitcast.4) | data formatting | bytes 1048576

commit v5 on v4

--- a/solution.py
+++ b/solution.py
@@ -45,16 +45,16 @@
     return code.astype(jnp.int32).astype(jnp.float32) * scale
 
 
-def kernel(n, ny, lists_s, order_s, lists_v, order_v, x_ref, a_ref, diag_ref, own, sum_ref,
-           pick, keep, local_pick, local_keep, a_top, a_low, g_ref, oth, recv, bbuf, mine, codes, scales, got_codes, got_scales, all_codes, all_scales, diag,
-           a_sem, loc_sem, diag_sem, z_send, z_recv, y_send, y_recv, s_send, s_recv,
+def kernel(n, ny, lists_ref, order_ref, x_ref, a_ref, diag_ref, own, sum_ref,
+           lists_s, order_s, lists_v, order_v, pick, keep, local_pick, local_keep, a_top, a_low, g_ref, oth, recv, bbuf, mine, codes, scales, got_codes, got_scales, all_codes, all_scales, diag,
+           t_sem, a_sem, loc_sem, diag_sem, z_send, z_recv, y_send, y_recv, s_send, s_recv,
            v_send, v_recv, o_sem, r_send, r_recv, rs_send, rs_recv, b_send, b_recv, bs_send, bs_recv):
     nz = n // ny
     span = g_ref.shape[3] * BLK // n
     rows = a_ref.shape[1]
     blocks_col = a_ref.shape[2] // BLK
     blocks_row = rows // BLK
-    tall = a_top.shape[2]
+    tall = a_top.shape[1]
     per = max(1, span // BLK)
     unit = min(span, BLK)
     row = lax.axis_index("row")
@@ -71,22 +71,9 @@
     def place(k, r):
         return aligned(k * n * size + r * size, size)
 
-    def stream(half, b):
+    def stream(half):
         a_half = a_low if half else a_top
-        return pltpu.make_async_copy(
-            a_ref.at[:, half * tall:(half + 1) * tall, aligned(b * BLK, BLK)], a_half.at[b], a_sem.at[half, b])
-
-    def start_stream(half):
-        def one(b, carry):
-            stream(half, b).start()
-            return carry
-        lax.fori_loop(0, blocks_col, one, 0)
-
-    def wait_stream(half):
-        def one(b, carry):
-            stream(half, b).wait()
-            return carry
-        lax.fori_loop(0, blocks_col, one, 0)
+        return pltpu.make_async_copy(a_ref.at[:, half * tall:(half + 1) * tall], a_half, a_sem.at[half])
 
     def slot(c, k, r):
         if span >= BLK:
@@ -101,8 +88,12 @@
 
     for k in range(NSN):
         local(k).start()
+    tables = [pltpu.make_async_copy(*pair, t_sem.at[i]) for i, pair in enumerate(
+        ((lists_ref, lists_s), (order_ref, order_s), (lists_ref, lists_v), (order_ref, order_v)))]
+    for c in tables:
+        c.start()
     for half in range(2):
-        start_stream(half)
+        stream(half).start()
 
     barrier = pltpu.get_barrier_semaphore()
     pl.semaphore_signal(barrier, inc=1, device_id=sibling, device_id_type=MESH)
@@ -141,6 +132,8 @@
         sib(x_ref.at[k], col, k, row).start()
     for k in range(NSN):
         own_diag(k).start()
+    for c in tables:
+        c.wait()
     index_tables(lists_s, order_s, lists_v, order_v, pick, keep, local_pick, local_keep,
                  col * blocks_col, row, blocks_col, blocks_row)
     own[...] = jnp.zeros_like(own)
@@ -198,8 +191,8 @@
             a_half = a_low if half else a_top
             pieces = []
             for e in range(per):
-                block = pick[k, (r * span + e * BLK) // BLK]
-                pieces += [a_half[block, 0], a_half[block, 1]]
+                block = pl.ds(pick[k, (r * span + e * BLK) // BLK] * BLK, BLK)
+                pieces += [a_half[0, :, block], a_half[1, :, block]]
             left.append(jnp.concatenate(pieces, axis=1))
         left = jnp.concatenate(left, axis=0) if len(left) > 1 else left[0]
         for rel in range(2):
@@ -258,8 +251,8 @@
         pl.when(z + d < nz)(lambda: from_line(k, z + d, z > 0, down))
         pl.when(z - d + 1 >= 0)(lambda: from_side(k, z - d + 1))
         pl.when((d > 1) & (z + d - 1 < nz))(lambda: from_side(k, z + d - 1))
-        pl.when(m == 0)(lambda: wait_stream(0))
-        pl.when(m == 2)(lambda: wait_stream(1))
+        pl.when(m == 0)(lambda: stream(0).wait())
+        pl.when(m == 2)(lambda: stream(1).wait())
         cut = NSN + 4
         low, high = jnp.where(m % 2 == 0, 0, cut), jnp.where(m % 2 == 0, cut, cut + 4)
         pl.when(m < 2)(lambda: entries(low, high, (0,), True))
@@ -386,15 +379,19 @@
     values, schur = pl.pallas_call(
         functools.partial(kernel, n, ny),
         out_shape=(pltpu.VMEM(side, jnp.float32), pltpu.VMEM((size, half), jnp.float32)),
-        in_specs=[SMEM, SMEM, VMEM, VMEM, ANY, ANY, ANY],
+        in_specs=[ANY, ANY, ANY, ANY, ANY],
         out_specs=(VMEM, VMEM),
         scratch_shapes=[
+            pltpu.SMEM((NSN, listed), jnp.int32),
+            pltpu.SMEM(order.shape, jnp.int32),
+            pltpu.VMEM((NSN, listed), jnp.int32),
+            pltpu.VMEM(order.shape, jnp.int32),
             pltpu.SMEM((NSN, listed), jnp.int32),
             pltpu.SMEM((NSN, listed), jnp.float32),
             pltpu.SMEM((NSN, blocks_row), jnp.int32),
             pltpu.SMEM((NSN, blocks_row), jnp.float32),
-            pltpu.VMEM((blocks_col, 2, rows // 2, BLK), jnp.bfloat16),
-            pltpu.VMEM((blocks_col, 2, rows // 2, BLK), jnp.bfloat16),
+            pltpu.VMEM((2, rows // 2, cols), jnp.bfloat16),
+            pltpu.VMEM((2, rows // 2, cols), jnp.bfloat16),
             pltpu.VMEM((2, NSN, 2, listed, BLK, half), jnp.bfloat16),
             pltpu.VMEM(side, jnp.float32),
             pltpu.VMEM(side, jnp.float32),
@@ -404,7 +401,7 @@
             pltpu.VMEM((NSN, n, piece, half), jnp.int16), pltpu.VMEM((NSN, n, 1, half), jnp.float32),
             pltpu.VMEM((NSN, n, piece, half), jnp.int16), pltpu.VMEM((NSN, n, 1, half), jnp.float32),
             pltpu.VMEM((NSN, piece, half), jnp.bfloat16),
-            dma((2, blocks_col)), dma((NSN,)), dma((NSN,)), dma((NSN, nz + 2)), dma((NSN, nz)),
+            dma((4,)), dma((2,)), dma((NSN,)), dma((NSN,)), dma((NSN, nz + 2)), dma((NSN, nz)),
             dma((NSN, nz)), dma((NSN, nz)), dma((NSN, n)), dma((NSN, n)),
             dma((NSN, blocks_row)), dma((NSN, blocks_row)), dma((NSN, blocks_row)),
             dma((NSN, n)), dma((NSN, n)), dma((NSN, n)), dma((NSN, n)),
@@ -413,7 +410,7 @@
         compiler_params=pltpu.CompilerParams(
             collective_id=0, has_side_effects=True, vmem_limit_bytes=58000000),
         name="inversion_step",
-    )(row_lists, order, row_lists, order, shards, inverse_pairs, diag_blocks.reshape(size, half))
+    )(row_lists, order, shards, inverse_pairs, diag_blocks.reshape(size, half))
     return (values, schur.reshape(diag_blocks.shape))
 
 

time: 59.6 us -> 56.1 us (0.941)
  Pallas kernels: 56.4 us -> 52.9 us
    pallas_call x1, Pallas kernels: 56.4 us -> 52.9 us  [local(): pl.pallas_call(functools.partial(kernel, n, ny), out_shape=(pltpu.VMEM(si...]
where the time goes in v5:
time: 56.1 us; the launch traced here: 56 us
  Pallas kernels  52.9 us (94%)
  local copies, waits for them, and re-layouts  2.46 us (4%)
  between operations  0.64 us (1%)
    pallas_call x1, Pallas kernels, local(): pl.pallas_call(functools.partial(kernel, n, ny), out_shape=(pltpu.VMEM(si...  52.9 us
    unnamed x2, local copies, waits for them, and re-layouts  2.46 us

profile of v5, /device:TPU:0, one launch (start us, length us, event | category | flops | bytes accessed | tf_op | source)
XLA Modules:
  0.0 56.0 jit_solution(10903164644090034359)
XLA Ops:
  0.6 52.9 %inversion_step.1 = (f32[2,2,1536,128]{3,2,1,0:T(8,128)S(1)}, f32[1024,128]{1,0:T(8,128)S(1)}) custom-call(s32[2,16]{1,0:T(2,128)} %lists_ref.1, s32[1,96]{1,0:T(1,128)} %bitcast.7, bf16[2,2,2,128,128]{4,3,2,1,0:T(8,128)(2,1)} %bitcast.5, bf16[2,1536,6144]{2,1,0:T(8,128)(2,1)} %a_ref.1, bf16[1024,128]{1,0:T(8,128)(2,1)} %bitcast.6), custom_call_target="tpu_custom_call" | custom-call | tf_op jit(solution)/shard_map/inversion_step/pallas_call | solution.py:379
  53.5 1.7 %copy.9 = f32[2,2,1536,128]{3,2,1,0:T(8,128)} copy(f32[2,2,1536,128]{3,2,1,0:T(8,128)S(1)} %get-tuple-element.6) | data formatting | bytes 6291456
  55.2 0.8 %copy.10 = f32[2,2,256,128]{3,2,1,0:T(8,128)} copy(f32[2,2,256,128]{3,2,1,0:T(8,128)S(1)} %bitcast.4) | data formatting | bytes 1048576

commit v6 on v5

--- a/solution.py
+++ b/solution.py
@@ -47,7 +47,7 @@
 
 def kernel(n, ny, lists_ref, order_ref, x_ref, a_ref, diag_ref, own, sum_ref,
            lists_s, order_s, lists_v, order_v, pick, keep, local_pick, local_keep, a_top, a_low, g_ref, oth, recv, bbuf, mine, codes, scales, got_codes, got_scales, all_codes, all_scales, diag,
-           t_sem, a_sem, loc_sem, diag_sem, z_send, z_recv, y_send, y_recv, s_send, s_recv,
+           t_sem, a_sem, loc_sem, diag_sem, z_send, z_recv, y_send, y_recv, x_send, s_send, s_recv,
            v_send, v_recv, o_sem, r_send, r_recv, rs_send, rs_recv, b_send, b_recv, bs_send, bs_recv):
     nz = n // ny
     span = g_ref.shape[3] * BLK // n
@@ -149,12 +149,31 @@
         def _():
             line(here(k, zz, y), k, zz, target).start()
 
-        side(here(k, zz, y), k, zz, y).start()
+        pl.when(crosses(k, zz))(lambda: side(here(k, zz, y), k, zz, y).start())
         sib(here(k, zz, y), col, k, zz * ny + y).start()
 
+    def crosses(k, zz):
+        return (k < NSN - 1) | ((zz > 0) & (zz < nz - 1))
+
+    def relay(end):
+        zz = end * (nz - 1)
+        return copy(here(NSN - 1, zz, oy), col, NSN - 1, zz * ny + oy, x_send.at[end], y_recv.at[NSN - 1, zz],
+                    down if end else up)
+
+    def arrived(k, zz):
+        side(here(k, zz, oy), k, zz, oy).wait_recv()
+        pl.when((k == NSN - 1) & (zz == 0) & (z < nz - 1))(lambda: relay(0).start())
+        pl.when((k == NSN - 1) & (zz == nz - 1) & (z > 0))(lambda: relay(1).start())
+        sib(here(k, zz, oy), col, k, zz * ny + oy).start()
+
     def from_side(k, zz):
-        side(here(k, zz, oy), k, zz, oy).wait_recv()
-        sib(here(k, zz, oy), col, k, zz * ny + oy).start()
+        pl.when((zz == z) | crosses(k, zz))(lambda: arrived(k, zz))
+
+    def from_relay(m):
+        for zz in (0, nz - 1):
+            away = jnp.abs(z - zz)
+            due = jnp.where(away < 3, away + 2, 2 * away + 1)
+            pl.when((away > 0) & (m == due))(lambda zz=zz: arrived(NSN - 1, zz))
 
     outs = (own, oth)
 
@@ -221,12 +240,9 @@
 
 
     steps = max(2 * nz, 4)
-    last = NSN + 4 * (steps - 1)
 
     def entries(low, high, halves, fresh):
         def entry(e, carry):
-            if len(halves) > 1:
-                pl.when(e == last)(lambda: start_swaps(0))
             g = (e - NSN) // 4
             q = (e - NSN) % 4
             away = g // 2 + 1 - q // 2
@@ -242,11 +258,12 @@
 
     def done_by(m):
         ahead = NSN + 4 * jnp.where(m >= steps - 2, m + 1, m)
-        return jnp.where(m < 3, NSN + 8, NSN + 4 * jnp.where(m >= steps - 1, m + 1, m))
+        return jnp.where(m < 3, NSN + 8, ahead)
 
     def step(m, carry):
         d = m // 2 + 1
         k = m % 2
+        from_relay(m)
         pl.when(z - d >= 0)(lambda: from_line(k, z - d, z < nz - 1, up))
         pl.when(z + d < nz)(lambda: from_line(k, z + d, z > 0, down))
         pl.when(z - d + 1 >= 0)(lambda: from_side(k, z - d + 1))
@@ -257,6 +274,7 @@
         low, high = jnp.where(m % 2 == 0, 0, cut), jnp.where(m % 2 == 0, cut, cut + 4)
         pl.when(m < 2)(lambda: entries(low, high, (0,), True))
         pl.when((m >= 2) & (m < 4))(lambda: entries(low, high, (1,), False))
+        pl.when(m == steps - 1)(lambda: start_swaps(0))
         entries(done_by(m - 1), done_by(m), (0, 1), True)
         return carry
 
@@ -335,11 +353,13 @@
             for c in spread(k, d, row):
                 c.start()
 
+    pl.when(z < nz - 1)(lambda: relay(0).wait_send())
+    pl.when(z > 0)(lambda: relay(1).wait_send())
     for k in range(NSN):
         for r in range(n):
             sib(slot(col, k, r), col, k, r).wait_send()
         for zz in range(nz):
-            side(here(k, zz, y), k, zz, y).wait_send()
+            pl.when((z == zz) | crosses(k, zz))(lambda k=k, zz=zz: side(here(k, zz, y), k, zz, y).wait_send())
             pl.when(((zz < z) & (z < nz - 1)) | ((zz > z) & (z > 0)))(
                 lambda k=k, zz=zz: line(here(k, zz, y), k, zz, up).wait_send())
         pl.when(z < nz - 1)(lambda k=k: first_up(k).wait_send())
@@ -402,7 +422,7 @@
             pltpu.VMEM((NSN, n, piece, half), jnp.int16), pltpu.VMEM((NSN, n, 1, half), jnp.float32),
             pltpu.VMEM((NSN, piece, half), jnp.bfloat16),
             dma((4,)), dma((2,)), dma((NSN,)), dma((NSN,)), dma((NSN, nz + 2)), dma((NSN, nz)),
-            dma((NSN, nz)), dma((NSN, nz)), dma((NSN, n)), dma((NSN, n)),
+            dma((NSN, nz)), dma((NSN, nz)), dma((2,)), dma((NSN, n)), dma((NSN, n)),
             dma((NSN, blocks_row)), dma((NSN, blocks_row)), dma((NSN, blocks_row)),
             dma((NSN, n)), dma((NSN, n)), dma((NSN, n)), dma((NSN, n)),
             dma((NSN, n)), dma((NSN, n)), dma((NSN, n)), dma((NSN, n)),

time: 56.1 us -> 55.5 us (0.989)
  Pallas kernels: 52.9 us -> 52.3 us
    pallas_call x1, Pallas kernels: 52.9 us -> 52.3 us  [local(): pl.pallas_call(functools.partial(kernel, n, ny), out_shape=(pltpu.VMEM(si...]
where the time goes in v6:
time: 55.5 us; the launch traced here: 55.4 us
  Pallas kernels  52.3 us (94%)
  local copies, waits for them, and re-layouts  2.46 us (4%)
  between operations  0.64 us (1%)
    pallas_call x1, Pallas kernels, local(): pl.pallas_call(functools.partial(kernel, n, ny), out_shape=(pltpu.VMEM(si...  52.3 us
    unnamed x2, local copies, waits for them, and re-layouts  2.46 us

profile of v6, /device:TPU:0, one launch (start us, length us, event | category | flops | bytes accessed | tf_op | source)
XLA Modules:
  0.0 55.4 jit_solution(17849483046749358151)
XLA Ops:
  0.6 52.3 %inversion_step.1 = (f32[2,2,1536,128]{3,2,1,0:T(8,128)S(1)}, f32[1024,128]{1,0:T(8,128)S(1)}) custom-call(s32[2,16]{1,0:T(2,128)} %lists_ref.1, s32[1,96]{1,0:T(1,128)} %bitcast.7, bf16[2,2,2,128,128]{4,3,2,1,0:T(8,128)(2,1)} %bitcast.5, bf16[2,1536,6144]{2,1,0:T(8,128)(2,1)} %a_ref.1, bf16[1024,128]{1,0:T(8,128)(2,1)} %bitcast.6), custom_call_target="tpu_custom_call" | custom-call | tf_op jit(solution)/shard_map/inversion_step/pallas_call | solution.py:399
  52.9 1.7 %copy.9 = f32[2,2,1536,128]{3,2,1,0:T(8,128)} copy(f32[2,2,1536,128]{3,2,1,0:T(8,128)S(1)} %get-tuple-element.6) | data formatting | bytes 6291456
  54.6 0.8 %copy.10 = f32[2,2,256,128]{3,2,1,0:T(8,128)} copy(f32[2,2,256,128]{3,2,1,0:T(8,128)S(1)} %bitcast.4) | data formatting | bytes 1048576

commit v7 on v6

--- a/solution.py
+++ b/solution.py
@@ -220,7 +220,7 @@
             outs[rel][k, 0, at, :] += found[:, :BLK]
             outs[rel][k, 1, at, :] += found[:, BLK:]
 
-    group = 3 if blocks_row % 3 == 0 else 1
+    group = 2 if blocks_row % 2 == 0 else 3 if blocks_row % 3 == 0 else 1
     strips = blocks_row // group
     high = group * BLK
 
@@ -323,13 +323,11 @@
                 right.append(jnp.concatenate([-imag, real], axis=1))
             factor = jnp.concatenate(left, axis=0)
             wide = jnp.concatenate(right, axis=0)
-            total = None
-            for _ in range(2):
-                piece = wide.astype(jnp.bfloat16)
-                wide = wide - piece.astype(jnp.float32)
-                term = lax.dot_general(factor, piece, (((0,), (0,)), ((), ())),
-                                       preferred_element_type=jnp.float32)
-                total = term if total is None else total + term
+            high_part = wide.astype(jnp.bfloat16)
+            low_part = (wide - high_part.astype(jnp.float32)).astype(jnp.bfloat16)
+            both = lax.dot_general(factor, jnp.concatenate([high_part, low_part], axis=1), (((0,), (0,)), ((), ())),
+                                   preferred_element_type=jnp.float32)
+            total = both[:, :width] + both[:, width:]
             mine[2 * k * width:(2 * k + 1) * width, :] += total[:, :BLK]
             mine[(2 * k + 1) * width:(2 * k + 2) * width, :] += total[:, BLK:]
             return carry

time: 55.5 us -> 55.8 us (level)
  no operation moved by 1% of the time
where the time goes in v7:
time: 55.8 us; the launch traced here: 55.9 us
  Pallas kernels  52.8 us (95%)
  local copies, waits for them, and re-layouts  2.46 us (4%)
  between operations  0.64 us (1%)
    pallas_call x1, Pallas kernels, local(): pl.pallas_call(functools.partial(kernel, n, ny), out_shape=(pltpu.VMEM(si...  52.8 us
    unnamed x2, local copies, waits for them, and re-layouts  2.46 us

profile of v7, /device:TPU:0, one launch (start us, length us, event | category | flops | bytes accessed | tf_op | source)
XLA Modules:
  0.0 55.9 jit_solution(16888840925583347460)
XLA Ops:
  0.6 52.8 %inversion_step.1 = (f32[2,2,1536,128]{3,2,1,0:T(8,128)S(1)}, f32[1024,128]{1,0:T(8,128)S(1)}) custom-call(s32[2,16]{1,0:T(2,128)} %lists_ref.1, s32[1,96]{1,0:T(1,128)} %bitcast.7, bf16[2,2,2,128,128]{4,3,2,1,0:T(8,128)(2,1)} %bitcast.5, bf16[2,1536,6144]{2,1,0:T(8,128)(2,1)} %a_ref.1, bf16[1024,128]{1,0:T(8,128)(2,1)} %bitcast.6), custom_call_target="tpu_custom_call" | custom-call | tf_op jit(solution)/shard_map/inversion_step/pallas_call | solution.py:397
  53.4 1.7 %copy.9 = f32[2,2,1536,128]{3,2,1,0:T(8,128)} copy(f32[2,2,1536,128]{3,2,1,0:T(8,128)S(1)} %get-tuple-element.6) | data formatting | bytes 6291456
  55.1 0.8 %copy.10 = f32[2,2,256,128]{3,2,1,0:T(8,128)} copy(f32[2,2,256,128]{3,2,1,0:T(8,128)S(1)} %bitcast.4) | data formatting | bytes 1048576
